TPU v7x, 32 devices: a whole 2x2x4 slice. The times are simulated.
32 devices in a mesh: song: 2 (over y), seq: 16 (over z, x, core).
Axes of the slice: x: 2, y: 2, z: 4, core: 2. Of those that a mesh axis runs over, the one named last changes fastest.
Arguments:
- song_ids: int32 [4096], P(('song', 'seq')), parts along dimension 0, may hold values from 0 to 2047
- table: bfloat16 [2048, 2432], P(None, 'seq'), may hold values from -6 to 6
- position_table: bfloat16 [2048, 2432], P('seq'), may hold values from -4 to 4
- w_qkv: bfloat16 [2, 2432, 1800], replicated, may hold values from -4 to 4
- w_out: bfloat16 [2, 600, 2432], replicated, may hold values from -0.25 to 0.25
Outputs:
- stream_out: bfloat16 [4096, 2432], P(('song', 'seq')), parts along dimension 0
There are 2 independent parts, one for each index of `song`. A program takes and returns all parts, laid end to end along the dimension named above; an argument that names none is the same for every part. Nothing has to cross between parts.
All inputs are finite; a program needn't handle non-finite values.
Results may differ from a plain program's by a relative error of at most 0.0065.
Values may be sent and summed in bfloat16 or wider, within the bound.
A program may use at most 192 MiB of HBM per device.

v0:
```python
import functools
import math

import jax
import jax.numpy as jnp
from jax import lax
from jax.experimental import pallas as pl
from jax.experimental.pallas import tpu as pltpu
from jax.sharding import PartitionSpec as P

HEADS = 4
HEAD = 150
MESH = pl.DeviceIdType.MESH

epsilon = 1e-05


def cuts(width, step):
    return [(a, min(a + step, width)) for a in range(0, width, step)]


def normalize_into(resid, normed):
    value = resid[...]
    mean = jnp.mean(value, axis=-1, keepdims=True)
    centered = value - mean
    variance = jnp.mean(centered * centered, axis=-1, keepdims=True)
    normed[...] = (centered * lax.rsqrt(variance + epsilon)).astype(jnp.bfloat16)


def dot_nt(a, b):
    dims = (((1,), (1,)), ((), ()))
    return lax.dot_general(a, b, dims, preferred_element_type=jnp.float32)


def scores_of(q, k):
    return dot_nt(q, k) * (1.0 / math.sqrt(HEAD))


def split_at(columns):
    return -(-columns // 2 // 128) * 128


def kernel(n, ids_hbm, table_hbm, pos_hbm, wqkv_hbm, wout_hbm, out_ref,
           pos_v, wq_v, wo_v, table_t, ids_all, emb_s, emb_r, emb_t, resid, normed,
           qkv_s0, qkv_s1, qkv_r0, qkv_r1, wide, mix_s0, mix_s1, mix_r0, mix_r1, mixed, kv_s, kv_r,
           load_sem, ids_ss, ids_rs, emb_ss, emb_rs, qkv_ss, qkv_rs, mix_ss, mix_rs, kv_ss, kv_rs):
    me = lax.axis_index("seq")
    features, vocab = table_t.shape
    tokens, depth = resid.shape
    cols = tokens // n
    width = wide.shape[1]
    att = mixed.shape[1]

    def peer_at(step):
        return lax.rem(me + 1 + lax.rem(n // 2 - 1 + step, n - 1), n)

    def each_peer(fn):
        def run(step, carry):
            fn(peer_at(step))
            return carry
        lax.fori_loop(0, n - 1, run, 0)

    def send(src, dst, ss, rs, peer):
        return pltpu.make_async_remote_copy(
            src_ref=src, dst_ref=dst.at[me], send_sem=ss.at[peer], recv_sem=rs.at[me],
            device_id={"seq": peer}, device_id_type=MESH)

    def arrival(src, dst, ss, rs, peer):
        return pltpu.make_async_remote_copy(
            src_ref=src, dst_ref=dst.at[peer], send_sem=ss.at[peer], recv_sem=rs.at[peer],
            device_id={"seq": peer}, device_id_type=MESH)

    loads = [pltpu.make_async_copy(table_hbm, table_t, load_sem.at[0]),
             pltpu.make_async_copy(pos_hbm, pos_v, load_sem.at[1])]
    for layer in range(2):
        loads.append(pltpu.make_async_copy(wqkv_hbm.at[layer], wq_v.at[layer], load_sem.at[2 + 2 * layer]))
        loads.append(pltpu.make_async_copy(wout_hbm.at[layer], wo_v.at[layer], load_sem.at[3 + 2 * layer]))
    own_ids = ids_all.at[me]
    ids_load = pltpu.make_async_copy(ids_hbm, own_ids, load_sem.at[6])
    ids_load.start()
    loads[0].start()

    barrier = pltpu.get_barrier_semaphore()
    each_peer(lambda peer: pl.semaphore_signal(barrier, inc=1, device_id={"seq": peer}, device_id_type=MESH))
    pl.semaphore_wait(barrier, n - 1)
    ids_load.wait()

    each_peer(lambda peer: send(own_ids, ids_all, ids_ss, ids_rs, peer).start())
    loads[0].wait()
    for load in loads[1:]:
        load.start()

    def gather(ids):
        codes = lax.broadcasted_iota(jnp.int32, (vocab, tokens), 0)
        hot = jnp.where(codes == ids, 1.0, 0.0).astype(jnp.bfloat16)
        return jnp.dot(table_t[...], hot, preferred_element_type=jnp.float32).astype(jnp.bfloat16)

    def serve(peer):
        arrival(own_ids, ids_all, ids_ss, ids_rs, peer).wait_recv()
        emb_s[peer] = gather(ids_all[peer])
        send(emb_s.at[peer], emb_r, emb_ss, emb_rs, peer).start()

    each_peer(serve)
    emb_r[me] = gather(ids_all[me])
    each_peer(lambda peer: arrival(emb_s.at[peer], emb_r, emb_ss, emb_rs, peer).wait_recv())
    for src in range(n):
        emb_t[src * features:(src + 1) * features, :] = emb_r[src].astype(jnp.float32)
    loads[1].wait()
    for a, b in cuts(depth, 128):
        resid[:, a:b] = emb_t[a:b, :].T + pos_v[:, a:b].astype(jnp.float32)

    normalize_into(resid, normed)
    loads[2].wait()
    qkv = [(0, split_at(width), qkv_s0, qkv_r0), (split_at(width), width, qkv_s1, qkv_r1)]
    for part, (a, b, out, got) in enumerate(qkv):
        wide[:, a:b] = dot_nt(normed[...], wq_v[0, a:b, :])
        for dst in range(n):
            out[dst] = wide[dst * cols:(dst + 1) * cols, a:b].astype(jnp.bfloat16)
        each_peer(lambda peer: send(out.at[peer], got, qkv_ss.at[part], qkv_rs.at[part], peer).start())
        got[me] = out[me]

    first = lax.broadcasted_iota(jnp.int32, (tokens, tokens), 0)
    second = lax.broadcasted_iota(jnp.int32, (tokens, tokens), 1)
    allowed = (((first - second) & (cols - 1)) == 0) & (second <= first)
    mix = [(0, split_at(att), mix_s0, mix_r0), (split_at(att), att, mix_s1, mix_r1)]
    ready = [0, 0]
    for h in range(HEADS):
        at = 3 * HEAD * h
        for part, (a, b, out, got) in enumerate(qkv):
            if not ready[part] and at + 3 * HEAD > a:
                ready[part] = 1
                each_peer(lambda peer: arrival(
                    out.at[peer], got, qkv_ss.at[part], qkv_rs.at[part], peer).wait_recv())
                for src in range(n):
                    wide[src * cols:(src + 1) * cols, a:b] = got[src].astype(jnp.float32)
        q = wide[:, at:at + HEAD].astype(jnp.bfloat16)
        k = wide[:, at + HEAD:at + 2 * HEAD].astype(jnp.bfloat16)
        v = wide[:, at + 2 * HEAD:at + 3 * HEAD].astype(jnp.bfloat16)
        scores = jnp.where(allowed, scores_of(q, k), -jnp.inf)
        lifted = jnp.exp(scores - jnp.max(scores, axis=-1, keepdims=True))
        probs = (lifted / jnp.sum(lifted, axis=-1, keepdims=True)).astype(jnp.bfloat16)
        mixed[:, HEAD * h:HEAD * (h + 1)] = jnp.dot(probs, v, preferred_element_type=jnp.float32)
        for part, (a, b, out, got) in enumerate(mix):
            if HEAD * h < b <= HEAD * (h + 1):
                for dst in range(n):
                    out[dst] = mixed[dst * cols:(dst + 1) * cols, a:b].astype(jnp.bfloat16)
                each_peer(lambda peer: send(out.at[peer], got, mix_ss.at[part], mix_rs.at[part], peer).start())
                got[me] = out[me]
    for part, (a, b, out, got) in enumerate(mix):
        each_peer(lambda peer: arrival(out.at[peer], got, mix_ss.at[part], mix_rs.at[part], peer).wait_recv())
        for src in range(n):
            mixed[src * cols:(src + 1) * cols, a:b] = got[src].astype(jnp.float32)

    loads[3].wait()
    back = mixed[...].astype(jnp.bfloat16)
    for a, b in cuts(depth, 512):
        resid[:, a:b] += jnp.dot(back, wo_v[0, :, a:b], preferred_element_type=jnp.float32)
    normalize_into(resid, normed)
    loads[4].wait()

    def shift(pair):
        return pltpu.make_async_remote_copy(
            src_ref=kv_s.at[pair], dst_ref=kv_r.at[pair], send_sem=kv_ss.at[pair], recv_sem=kv_rs.at[pair],
            device_id={"seq": lax.rem(me + 1, n)}, device_id_type=MESH)

    @pl.when(me == 0)
    def _():
        kv_r[...] = jnp.zeros_like(kv_r)

    done = 0
    for pair in range(2):
        until = -(-3 * HEAD * (HEADS // 2) * (pair + 1) // 128) * 128 if pair == 0 else width
        for a, b in cuts(until - done, 512):
            a, b = a + done, b + done
            wide[:, a:b] = dot_nt(normed[...], wq_v[1, a:b, :])
        done = until
        for i in range(HEADS // 2):
            at = 3 * HEAD * (pair * (HEADS // 2) + i) + HEAD
            kv_s[pair, :, 2 * HEAD * i:2 * HEAD * (i + 1)] = wide[:, at:at + 2 * HEAD].astype(jnp.bfloat16)

        @pl.when(me < n - 1)
        def _():
            shift(pair).start()

    for h in range(HEADS):
        pair, i = divmod(h, HEADS // 2)
        if i == 0:
            @pl.when(me > 0)
            def _():
                shift(pair).wait_recv()
        at = 3 * HEAD * h
        q = wide[:, at:at + HEAD].astype(jnp.bfloat16)
        k_own = wide[:, at + HEAD:at + 2 * HEAD].astype(jnp.bfloat16).astype(jnp.float32)
        v_own = wide[:, at + 2 * HEAD:at + 3 * HEAD].astype(jnp.bfloat16).astype(jnp.float32)
        k = kv_r[pair, :, 2 * HEAD * i:2 * HEAD * i + HEAD]
        v = kv_r[pair, :, 2 * HEAD * i + HEAD:2 * HEAD * (i + 1)]
        own = jnp.sum(q.astype(jnp.float32) * k_own, axis=-1, keepdims=True) * (1.0 / math.sqrt(HEAD))
        far = jnp.where(me > 0, scores_of(q, k), -jnp.inf)
        top = jnp.maximum(jnp.max(far, axis=-1, keepdims=True), own)
        far_lifted = jnp.exp(far - top)
        own_lifted = jnp.exp(own - top)
        total = jnp.sum(far_lifted, axis=-1, keepdims=True) + own_lifted
        far_probs = (far_lifted / total).astype(jnp.bfloat16)
        own_probs = (own_lifted / total).astype(jnp.bfloat16).astype(jnp.float32)
        mixed[:, HEAD * h:HEAD * (h + 1)] = (
            jnp.dot(far_probs, v, preferred_element_type=jnp.float32) + own_probs * v_own)

    loads[5].wait()
    back = mixed[...].astype(jnp.bfloat16)
    for a, b in cuts(depth, 512):
        out_ref[:, a:b] = (resid[:, a:b] + jnp.dot(
            back, wo_v[1, :, a:b], preferred_element_type=jnp.float32)).astype(jnp.bfloat16)

    def finish(peer):
        send(own_ids, ids_all, ids_ss, ids_rs, peer).wait_send()
        send(emb_s.at[peer], emb_r, emb_ss, emb_rs, peer).wait_send()
        for part in range(2):
            _, _, out, got = qkv[part]
            send(out.at[peer], got, qkv_ss.at[part], qkv_rs.at[part], peer).wait_send()
            _, _, out, got = mix[part]
            send(out.at[peer], got, mix_ss.at[part], mix_rs.at[part], peer).wait_send()

    each_peer(finish)

    @pl.when(me < n - 1)
    def _():
        shift(0).wait_send()
        shift(1).wait_send()


def solution(mesh):
    n = mesh.shape["seq"]

    def shards(song_ids, table, position_table, w_qkv, w_out):
        tokens, depth = position_table.shape
        vocab, features = table.shape
        layers, _, width = w_qkv.shape
        att = w_out.shape[1]
        cols = tokens // n
        bf16, f32 = jnp.bfloat16, jnp.float32
        peers = pltpu.SemaphoreType.DMA((n,))
        pairs = pltpu.SemaphoreType.DMA((2, n))
        hbm = pl.BlockSpec(memory_space=pl.ANY)
        return pl.pallas_call(
            functools.partial(kernel, n),
            out_shape=pltpu.VMEM((tokens, depth), bf16),
            in_specs=[hbm, hbm, hbm, hbm, hbm],
            out_specs=pl.BlockSpec(memory_space=pltpu.VMEM),
            scratch_shapes=[
                pltpu.VMEM((tokens, depth), bf16),
                pltpu.VMEM((layers, width, depth), bf16),
                pltpu.VMEM((layers, att, depth), bf16),
                pltpu.VMEM((features, vocab), bf16),
                pltpu.VMEM((n, 1, tokens), jnp.int32),
                pltpu.VMEM((n, features, tokens), bf16),
                pltpu.VMEM((n, features, tokens), bf16),
                pltpu.VMEM((depth, tokens), f32),
                pltpu.VMEM((tokens, depth), f32),
                pltpu.VMEM((tokens, depth), bf16),
                pltpu.VMEM((n, cols, split_at(width)), bf16),
                pltpu.VMEM((n, cols, width - split_at(width)), bf16),
                pltpu.VMEM((n, cols, split_at(width)), bf16),
                pltpu.VMEM((n, cols, width - split_at(width)), bf16),
                pltpu.VMEM((tokens, width), f32),
                pltpu.VMEM((n, cols, split_at(att)), bf16),
                pltpu.VMEM((n, cols, att - split_at(att)), bf16),
                pltpu.VMEM((n, cols, split_at(att)), bf16),
                pltpu.VMEM((n, cols, att - split_at(att)), bf16),
                pltpu.VMEM((tokens, att), f32),
                pltpu.VMEM((2, tokens, att), bf16),
                pltpu.VMEM((2, tokens, att), bf16),
                pltpu.SemaphoreType.DMA((7,)),
                peers, peers, peers, peers, pairs, pairs, pairs, pairs,
                pltpu.SemaphoreType.DMA((2,)),
                pltpu.SemaphoreType.DMA((2,)),
            ],
            compiler_params=pltpu.CompilerParams(
                collective_id=0, has_side_effects=True, vmem_limit_bytes=56 << 20),
            name="music_rows",
        )(song_ids.reshape(1, tokens), table.T, position_table, jnp.swapaxes(w_qkv, 1, 2), w_out)

    in_specs = (P(("song", "seq")), P(None, "seq"), P("seq", None), P(), P())
    out_specs = P(("song", "seq"), None)
    return jax.shard_map(shards, mesh=mesh, in_specs=in_specs, out_specs=out_specs, check_vma=False)
```

profile of v0, /device:TPU:12, one launch (start us, length us, event | category | flops | bytes accessed | tf_op | source)
XLA Modules:
  0.0 56.1 jit_solution(9481086006991999659)
XLA Ops:
  0.0 55.2 %music_rows.1 = bf16[128,2432]{1,0:T(8,128)(2,1)S(1)} custom-call(s32[1,128]{1,0:T(1,128)} %bitcast.5, bf16[152,2048]{1,0:T(8,128)(2,1)} %bitcast.4, bf16[128,2432]{1,0:T(8,128)(2,1)} %pos_hbm.1, bf16[2,1800,2432]{2,1,0:T(8,128)(2,1)} %bitcast.3, bf16[2,600,2432]{2,1,0:T(8,128)(2,1)} %wout_hbm.1), custom_call_target="tpu_custom_call" | custom-call | tf_op jit(solution)/shard_map/music_rows/pallas_call | solution.py:244
  55.2 0.8 %copy.7 = bf16[128,2432]{1,0:T(8,128)(2,1)} copy(bf16[128,2432]{1,0:T(8,128)(2,1)S(1)} %music_rows.1) | data formatting | bytes 1245184
where the time goes:
time: 56.2 us; the launch traced here: 56.1 us
  Pallas kernels  55.2 us (98%)
  local copies, waits for them, and re-layouts  0.83 us (1%)
    pallas_call x1, Pallas kernels, shards(): pl.pallas_call(functools.partial(kernel, n), out_shape=pltpu.VMEM((tokens...  55.2 us

commit v1 on v0

v1 whole, which is shorter than its diff:
```python
import functools
import math

import jax
import jax.numpy as jnp
from jax import lax
from jax.experimental import pallas as pl
from jax.experimental.pallas import tpu as pltpu
from jax.sharding import PartitionSpec as P

HEADS = 4
HEAD = 150
MESH = pl.DeviceIdType.MESH

epsilon = 1e-05
inv_root = 1.0 / math.sqrt(HEAD)


def cuts(width, step):
    return [(a, min(a + step, width)) for a in range(0, width, step)]


def spans(edges):
    return list(zip(edges[:-1], edges[1:]))


def qkv_spans(width):
    return spans([0] + [min(-(-3 * HEAD * (h + 1) // 128) * 128, width) for h in range(HEADS)])


def mix_spans(att):
    edges = [0, 2 * HEAD // 128 * 128, 3 * HEAD // 128 * 128, att]
    return spans(edges)


def normalize_into(resid, normed):
    value = resid[...]
    mean = jnp.mean(value, axis=-1, keepdims=True)
    centered = value - mean
    variance = jnp.mean(centered * centered, axis=-1, keepdims=True)
    normed[...] = (centered * lax.rsqrt(variance + epsilon)).astype(jnp.bfloat16)


def dot_nt(a, b):
    dims = (((1,), (1,)), ((), ()))
    return lax.dot_general(a, b, dims, preferred_element_type=jnp.float32)


def scores_of(q, k):
    return dot_nt(q, k) * inv_root


def kernel(n, ids_hbm, table_hbm, pos_hbm, wqkv_hbm, wout_hbm, out_ref,
           pos_v, wq_v, wo_v, table_t, ids_all, emb_s, emb_r, emb_t, resid, normed,
           qkv_s, qkv_r, wide, mix_s, mix_r, mixed, kv_s, kv_r,
           load_sem, ids_ss, ids_rs, emb_ss, emb_rs, qkv_ss, qkv_rs, mix_ss, mix_rs, kv_ss, kv_rs):
    me = lax.axis_index("seq")
    features, vocab = table_t.shape
    tokens, depth = resid.shape
    cols = tokens // n
    width = wide.shape[1]
    att = mixed.shape[1]
    others = list(range(n // 2, n)) + list(range(1, n // 2))

    def send(src, dst, ss, rs, k):
        return pltpu.make_async_remote_copy(
            src_ref=src, dst_ref=dst, send_sem=ss, recv_sem=rs,
            device_id={"seq": me ^ k}, device_id_type=MESH)

    def settle(ref, sem):
        pltpu.make_async_copy(ref, ref, sem).wait()

    def settle_all(ref, sem):
        settle(ref.at[pl.ds(0, n - 1)], sem)

    loads = [pltpu.make_async_copy(table_hbm, table_t, load_sem.at[0]),
             pltpu.make_async_copy(pos_hbm, pos_v, load_sem.at[1])]
    for layer in range(2):
        loads.append(pltpu.make_async_copy(wqkv_hbm.at[layer], wq_v.at[layer], load_sem.at[2 + 2 * layer]))
        loads.append(pltpu.make_async_copy(wout_hbm.at[layer], wo_v.at[layer], load_sem.at[3 + 2 * layer]))
    own_ids = ids_all.at[me]
    ids_load = pltpu.make_async_copy(ids_hbm, own_ids, load_sem.at[6])
    ids_load.start()
    loads[0].start()

    barrier = pltpu.get_barrier_semaphore()
    for k in others:
        pl.semaphore_signal(barrier, inc=1, device_id={"seq": me ^ k}, device_id_type=MESH)
    ids_load.wait()
    pl.semaphore_wait(barrier, n - 1)

    for k in others:
        send(own_ids, own_ids, ids_ss, ids_rs.at[k], k).start()
    loads[0].wait()
    for load in loads[1:]:
        load.start()

    def gather(ids):
        codes = lax.broadcasted_iota(jnp.int32, (vocab, tokens), 0)
        hot = jnp.where(codes == ids, 1.0, 0.0).astype(jnp.bfloat16)
        return jnp.dot(table_t[...], hot, preferred_element_type=jnp.float32).astype(jnp.bfloat16)

    def serve(step, carry):
        k = 1 + lax.rem(n // 2 - 1 + step, n - 1)
        peer = me ^ k
        settle(ids_all.at[peer], ids_rs.at[k])
        emb_s[peer] = gather(ids_all[peer])
        send(emb_s.at[peer], emb_r.at[me], emb_ss, emb_rs, k).start()
        return carry

    lax.fori_loop(0, n - 1, serve, 0)
    emb_r[me] = gather(ids_all[me])
    settle_all(emb_r, emb_rs)
    for src in range(n):
        emb_t[src * features:(src + 1) * features, :] = emb_r[src].astype(jnp.float32)
    loads[1].wait()
    for a, b in cuts(depth, 128):
        resid[:, a:b] = emb_t[a:b, :].T + pos_v[:, a:b].astype(jnp.float32)

    normalize_into(resid, normed)
    loads[2].wait()
    qkv = qkv_spans(width)
    for part, (a, b) in enumerate(qkv):
        wide[:, a:b] = dot_nt(normed[...], wq_v[0, a:b, :])
        for dst in range(n):
            qkv_s[part][dst] = wide[dst * cols:(dst + 1) * cols, a:b].astype(jnp.bfloat16)
        for k in others:
            send(qkv_s[part].at[me ^ k], qkv_r[part].at[me], qkv_ss.at[part], qkv_rs.at[part], k).start()
        qkv_r[part][me] = qkv_s[part][me]

    first = lax.broadcasted_iota(jnp.int32, (tokens, tokens), 0)
    second = lax.broadcasted_iota(jnp.int32, (tokens, tokens), 1)
    allowed = (((first - second) & (cols - 1)) == 0) & (second <= first)
    mix = mix_spans(att)
    sent = 0
    for h in range(HEADS):
        a, b = qkv[h]
        settle_all(qkv_r[h], qkv_rs.at[h])
        for src in range(n):
            wide[src * cols:(src + 1) * cols, a:b] = qkv_r[h][src].astype(jnp.float32)
        at = 3 * HEAD * h
        q = wide[:, at:at + HEAD].astype(jnp.bfloat16)
        k = wide[:, at + HEAD:at + 2 * HEAD].astype(jnp.bfloat16)
        v = wide[:, at + 2 * HEAD:at + 3 * HEAD].astype(jnp.bfloat16)
        scores = jnp.where(allowed, scores_of(q, k), -jnp.inf)
        lifted = jnp.exp(scores - jnp.max(scores, axis=-1, keepdims=True))
        probs = (lifted / jnp.sum(lifted, axis=-1, keepdims=True)).astype(jnp.bfloat16)
        mixed[:, HEAD * h:HEAD * (h + 1)] = jnp.dot(probs, v, preferred_element_type=jnp.float32)
        while sent < len(mix) and mix[sent][1] <= HEAD * (h + 1):
            a, b = mix[sent]
            for dst in range(n):
                mix_s[sent][dst] = mixed[dst * cols:(dst + 1) * cols, a:b].astype(jnp.bfloat16)
            for k in others:
                send(mix_s[sent].at[me ^ k], mix_r[sent].at[me], mix_ss.at[sent], mix_rs.at[sent], k).start()
            mix_r[sent][me] = mix_s[sent][me]
            sent += 1

    def receive_mix(part):
        a, b = mix[part]
        settle_all(mix_r[part], mix_rs.at[part])
        for src in range(n):
            mixed[src * cols:(src + 1) * cols, a:b] = mix_r[part][src].astype(jnp.float32)

    loads[3].wait()
    for parts in ((0,), tuple(range(1, len(mix)))):
        for part in parts:
            receive_mix(part)
        lo, hi = mix[parts[0]][0], mix[parts[-1]][1]
        back = mixed[:, lo:hi].astype(jnp.bfloat16)
        for a, b in cuts(depth, 512):
            resid[:, a:b] += jnp.dot(back, wo_v[0, lo:hi, a:b], preferred_element_type=jnp.float32)
    normalize_into(resid, normed)
    loads[4].wait()

    def shift(part):
        return pltpu.make_async_remote_copy(
            src_ref=kv_s[part], dst_ref=kv_r[part], send_sem=kv_ss.at[part], recv_sem=kv_rs.at[part],
            device_id={"seq": lax.rem(me + 1, n)}, device_id_type=MESH)

    @pl.when(me == 0)
    def _():
        for part in range(HEADS):
            kv_r[part][...] = jnp.zeros_like(kv_r[part])

    for part, (a, b) in enumerate(qkv):
        wide[:, a:b] = dot_nt(normed[...], wq_v[1, a:b, :])
        at = 3 * HEAD * part + HEAD
        kv_s[part][...] = wide[:, at:at + 2 * HEAD].astype(jnp.bfloat16)

        @pl.when(me < n - 1)
        def _():
            shift(part).start()

    owns = []
    for h in range(HEADS):
        at = 3 * HEAD * h
        q = wide[:, at:at + HEAD].astype(jnp.bfloat16)
        k_own = wide[:, at + HEAD:at + 2 * HEAD].astype(jnp.bfloat16).astype(jnp.float32)
        own = jnp.sum(q.astype(jnp.float32) * k_own, axis=-1, keepdims=True) * inv_root
        owns.append(own)

    loads[5].wait()
    for h in range(HEADS):
        @pl.when(me > 0)
        def _():
            shift(h).wait_recv()
        at = 3 * HEAD * h
        q = wide[:, at:at + HEAD].astype(jnp.bfloat16)
        v_own = wide[:, at + 2 * HEAD:at + 3 * HEAD].astype(jnp.bfloat16).astype(jnp.float32)
        k = kv_r[h][:, :HEAD]
        v = kv_r[h][:, HEAD:]
        own = owns[h]
        far = jnp.where(me > 0, scores_of(q, k), -jnp.inf)
        top = jnp.maximum(jnp.max(far, axis=-1, keepdims=True), own)
        far_lifted = jnp.exp(far - top)
        own_lifted = jnp.exp(own - top)
        total = jnp.sum(far_lifted, axis=-1, keepdims=True) + own_lifted
        far_probs = (far_lifted / total).astype(jnp.bfloat16)
        own_probs = (own_lifted / total).astype(jnp.bfloat16).astype(jnp.float32)
        mixed[:, HEAD * h:HEAD * (h + 1)] = (
            jnp.dot(far_probs, v, preferred_element_type=jnp.float32) + own_probs * v_own)
        if h == 1:
            lo, hi = mix[0]
            back = mixed[:, lo:hi].astype(jnp.bfloat16)
            for a, b in cuts(depth, 512):
                resid[:, a:b] += jnp.dot(back, wo_v[1, lo:hi, a:b], preferred_element_type=jnp.float32)

    lo, hi = mix[1][0], mix[-1][1]
    back = mixed[:, lo:hi].astype(jnp.bfloat16)
    for a, b in cuts(depth, 512):
        out_ref[:, a:b] = (resid[:, a:b] + jnp.dot(
            back, wo_v[1, lo:hi, a:b], preferred_element_type=jnp.float32)).astype(jnp.bfloat16)

    settle_all(ids_all, ids_ss)
    settle_all(emb_s, emb_ss)
    for part in range(HEADS):
        settle_all(qkv_s[part], qkv_ss.at[part])
    for part in range(len(mix)):
        settle_all(mix_s[part], mix_ss.at[part])

    @pl.when(me < n - 1)
    def _():
        for part in range(HEADS):
            shift(part).wait_send()


def solution(mesh):
    n = mesh.shape["seq"]

    def shards(song_ids, table, position_table, w_qkv, w_out):
        tokens, depth = position_table.shape
        vocab, features = table.shape
        layers, _, width = w_qkv.shape
        att = w_out.shape[1]
        cols = tokens // n
        bf16, f32 = jnp.bfloat16, jnp.float32
        hbm = pl.BlockSpec(memory_space=pl.ANY)
        qkv = [pltpu.VMEM((n, cols, b - a), bf16) for a, b in qkv_spans(width)]
        mix = [pltpu.VMEM((n, cols, b - a), bf16) for a, b in mix_spans(att)]
        kv = [pltpu.VMEM((tokens, 2 * HEAD), bf16)] * HEADS
        sems = pltpu.SemaphoreType.DMA
        return pl.pallas_call(
            functools.partial(kernel, n),
            out_shape=pltpu.VMEM((tokens, depth), bf16),
            in_specs=[hbm, hbm, hbm, hbm, hbm],
            out_specs=pl.BlockSpec(memory_space=pltpu.VMEM),
            scratch_shapes=[
                pltpu.VMEM((tokens, depth), bf16),
                pltpu.VMEM((layers, width, depth), bf16),
                pltpu.VMEM((layers, att, depth), bf16),
                pltpu.VMEM((features, vocab), bf16),
                pltpu.VMEM((n, 1, tokens), jnp.int32),
                pltpu.VMEM((n, features, tokens), bf16),
                pltpu.VMEM((n, features, tokens), bf16),
                pltpu.VMEM((depth, tokens), f32),
                pltpu.VMEM((tokens, depth), f32),
                pltpu.VMEM((tokens, depth), bf16),
                qkv, list(qkv),
                pltpu.VMEM((tokens, width), f32),
                mix, list(mix),
                pltpu.VMEM((tokens, att), f32),
                kv, list(kv),
                sems((7,)),
                sems, sems((n,)), sems, sems,
                sems((HEADS,)), sems((HEADS,)), sems((len(mix),)), sems((len(mix),)),
                sems((HEADS,)), sems((HEADS,)),
            ],
            compiler_params=pltpu.CompilerParams(
                collective_id=0, has_side_effects=True, vmem_limit_bytes=56 << 20),
            name="music_rows",
        )(song_ids.reshape(1, tokens), table.T, position_table, jnp.swapaxes(w_qkv, 1, 2), w_out)

    in_specs = (P(("song", "seq")), P(None, "seq"), P("seq", None), P(), P())
    out_specs = P(("song", "seq"), None)
    return jax.shard_map(shards, mesh=mesh, in_specs=in_specs, out_specs=out_specs, check_vma=False)
```

time: 56.2 us -> 52 us (0.925)
  Pallas kernels: 55.2 us -> 51 us
    pallas_call x1, Pallas kernels: 55.2 us -> 51 us  [shards(): pl.pallas_call(functools.partial(kernel, n), out_shape=pltpu.VMEM((tokens...]
where the time goes in v1:
time: 52 us; the launch traced here: 51.8 us
  Pallas kernels  51 us (98%)
  local copies, waits for them, and re-layouts  0.83 us (2%)
    pallas_call x1, Pallas kernels, shards(): pl.pallas_call(functools.partial(kernel, n), out_shape=pltpu.VMEM((tokens...  51 us

profile of v1, /device:TPU:12, one launch (start us, length us, event | category | flops | bytes accessed | tf_op | source)
XLA Modules:
  0.0 51.8 jit_solution(13118763077915557971)
XLA Ops:
  0.0 51.0 %music_rows.1 = bf16[128,2432]{1,0:T(8,128)(2,1)S(1)} custom-call(s32[1,128]{1,0:T(1,128)} %bitcast.5, bf16[152,2048]{1,0:T(8,128)(2,1)} %bitcast.4, bf16[128,2432]{1,0:T(8,128)(2,1)} %pos_hbm.1, bf16[2,1800,2432]{2,1,0:T(8,128)(2,1)} %bitcast.3, bf16[2,600,2432]{2,1,0:T(8,128)(2,1)} %wout_hbm.1), custom_call_target="tpu_custom_call" | custom-call | tf_op jit(solution)/shard_map/music_rows/pallas_call | solution.py:262
  51.0 0.8 %copy.7 = bf16[128,2432]{1,0:T(8,128)(2,1)} copy(bf16[128,2432]{1,0:T(8,128)(2,1)S(1)} %music_rows.1) | data formatting | bytes 1245184

commit v2 on v1

--- a/solution.py
+++ b/solution.py
@@ -24,13 +24,17 @@
     return list(zip(edges[:-1], edges[1:]))
 
 
+def head_spans(width):
+    return spans([0] + [min(-(-3 * HEAD * (h + 1) // 128) * 128, width) for h in range(HEADS)])
+
+
 def qkv_spans(width):
-    return spans([0] + [min(-(-3 * HEAD * (h + 1) // 128) * 128, width) for h in range(HEADS)])
+    heads = head_spans(width)
+    return [(heads[h][0], heads[h + 1][1]) for h in range(0, HEADS, 2)]
 
 
 def mix_spans(att):
-    edges = [0, 2 * HEAD // 128 * 128, 3 * HEAD // 128 * 128, att]
-    return spans(edges)
+    return spans([0, 2 * HEAD // 128 * 128, att])
 
 
 def normalize_into(resid, normed):
@@ -52,7 +56,7 @@
 
 def kernel(n, ids_hbm, table_hbm, pos_hbm, wqkv_hbm, wout_hbm, out_ref,
            pos_v, wq_v, wo_v, table_t, ids_all, emb_s, emb_r, emb_t, resid, normed,
-           qkv_s, qkv_r, wide, mix_s, mix_r, mixed, kv_s, kv_r,
+           qkv_s, qkv_r, wt, wide, mix_s, mix_r, mixed, kv_s, kv_r,
            load_sem, ids_ss, ids_rs, emb_ss, emb_rs, qkv_ss, qkv_rs, mix_ss, mix_rs, kv_ss, kv_rs):
     me = lax.axis_index("seq")
     features, vocab = table_t.shape
@@ -61,6 +65,7 @@
     width = wide.shape[1]
     att = mixed.shape[1]
     others = list(range(n // 2, n)) + list(range(1, n // 2))
+    parity = me & 1
 
     def send(src, dst, ss, rs, k):
         return pltpu.make_async_remote_copy(
@@ -101,15 +106,39 @@
         return jnp.dot(table_t[...], hot, preferred_element_type=jnp.float32).astype(jnp.bfloat16)
 
     def serve(step, carry):
-        k = 1 + lax.rem(n // 2 - 1 + step, n - 1)
+        group, turn = step // (n // 2), lax.rem(step, n // 2)
+        k = 2 * lax.rem(turn + n // 4, n // 2) + (group ^ parity)
         peer = me ^ k
-        settle(ids_all.at[peer], ids_rs.at[k])
+
+        @pl.when(k > 0)
+        def _():
+            settle(ids_all.at[peer], ids_rs.at[k])
+
         emb_s[peer] = gather(ids_all[peer])
-        send(emb_s.at[peer], emb_r.at[me], emb_ss, emb_rs, k).start()
+
+        @pl.when(k > 0)
+        def _():
+            send(emb_s.at[peer], emb_r.at[me], emb_ss, emb_rs, k).start()
         return carry
 
-    lax.fori_loop(0, n - 1, serve, 0)
-    emb_r[me] = gather(ids_all[me])
+    lax.fori_loop(0, n, serve, 0)
+    emb_r[me] = emb_s[me]
+
+    def turn_weights():
+        loads[4].wait()
+
+        def strip(i, carry):
+            at = pl.multiple_of(i * 128, 128)
+            for a, b in cuts(width, 128):
+                wt[pl.ds(at, 128), a:b] = wq_v[1, a:b, pl.ds(at, 128)].T
+            return carry
+
+        lax.fori_loop(0, depth // 128, strip, 0)
+
+    @pl.when(parity == 1)
+    def _():
+        turn_weights()
+
     settle_all(emb_r, emb_rs)
     for src in range(n):
         emb_t[src * features:(src + 1) * features, :] = emb_r[src].astype(jnp.float32)
@@ -128,16 +157,22 @@
             send(qkv_s[part].at[me ^ k], qkv_r[part].at[me], qkv_ss.at[part], qkv_rs.at[part], k).start()
         qkv_r[part][me] = qkv_s[part][me]
 
+    @pl.when(parity == 0)
+    def _():
+        turn_weights()
+
     first = lax.broadcasted_iota(jnp.int32, (tokens, tokens), 0)
     second = lax.broadcasted_iota(jnp.int32, (tokens, tokens), 1)
     allowed = (((first - second) & (cols - 1)) == 0) & (second <= first)
     mix = mix_spans(att)
     sent = 0
     for h in range(HEADS):
-        a, b = qkv[h]
-        settle_all(qkv_r[h], qkv_rs.at[h])
-        for src in range(n):
-            wide[src * cols:(src + 1) * cols, a:b] = qkv_r[h][src].astype(jnp.float32)
+        if h % 2 == 0:
+            part = h // 2
+            a, b = qkv[part]
+            settle_all(qkv_r[part], qkv_rs.at[part])
+            for src in range(n):
+                wide[src * cols:(src + 1) * cols, a:b] = qkv_r[part][src].astype(jnp.float32)
         at = 3 * HEAD * h
         q = wide[:, at:at + HEAD].astype(jnp.bfloat16)
         k = wide[:, at + HEAD:at + 2 * HEAD].astype(jnp.bfloat16)
@@ -170,7 +205,6 @@
         for a, b in cuts(depth, 512):
             resid[:, a:b] += jnp.dot(back, wo_v[0, lo:hi, a:b], preferred_element_type=jnp.float32)
     normalize_into(resid, normed)
-    loads[4].wait()
 
     def shift(part):
         return pltpu.make_async_remote_copy(
@@ -182,8 +216,8 @@
         for part in range(HEADS):
             kv_r[part][...] = jnp.zeros_like(kv_r[part])
 
-    for part, (a, b) in enumerate(qkv):
-        wide[:, a:b] = dot_nt(normed[...], wq_v[1, a:b, :])
+    for part, (a, b) in enumerate(head_spans(width)):
+        wide[:, a:b] = jnp.dot(normed[...], wt[:, a:b], preferred_element_type=jnp.float32)
         at = 3 * HEAD * part + HEAD
         kv_s[part][...] = wide[:, at:at + 2 * HEAD].astype(jnp.bfloat16)
 
@@ -233,7 +267,7 @@
 
     settle_all(ids_all, ids_ss)
     settle_all(emb_s, emb_ss)
-    for part in range(HEADS):
+    for part in range(len(qkv)):
         settle_all(qkv_s[part], qkv_ss.at[part])
     for part in range(len(mix)):
         settle_all(mix_s[part], mix_ss.at[part])
@@ -276,13 +310,14 @@
                 pltpu.VMEM((tokens, depth), f32),
                 pltpu.VMEM((tokens, depth), bf16),
                 qkv, list(qkv),
+                pltpu.VMEM((depth, width), bf16),
                 pltpu.VMEM((tokens, width), f32),
                 mix, list(mix),
                 pltpu.VMEM((tokens, att), f32),
                 kv, list(kv),
                 sems((7,)),
                 sems, sems((n,)), sems, sems,
-                sems((HEADS,)), sems((HEADS,)), sems((len(mix),)), sems((len(mix),)),
+                sems((len(qkv),)), sems((len(qkv),)), sems((len(mix),)), sems((len(mix),)),
                 sems((HEADS,)), sems((HEADS,)),
             ],
             compiler_params=pltpu.CompilerParams(

time: 52 us -> 50 us (0.962)
  Pallas kernels: 51 us -> 49 us
    pallas_call x1, Pallas kernels: 51 us -> 49 us  [shards(): pl.pallas_call(functools.partial(kernel, n), out_shape=pltpu.VMEM((tokens...]
where the time goes in v2:
time: 50 us; the launch traced here: 49.8 us
  Pallas kernels  49 us (98%)
  local copies, waits for them, and re-layouts  0.83 us (2%)
    pallas_call x1, Pallas kernels, shards(): pl.pallas_call(functools.partial(kernel, n), out_shape=pltpu.VMEM((tokens...  49 us

profile of v2, /device:TPU:12, one launch (start us, length us, event | category | flops | bytes accessed | tf_op | source)
XLA Modules:
  0.0 49.8 jit_solution(6607611156369003564)
XLA Ops:
  0.0 49.0 %music_rows.1 = bf16[128,2432]{1,0:T(8,128)(2,1)S(1)} custom-call(s32[1,128]{1,0:T(1,128)} %bitcast.5, bf16[152,2048]{1,0:T(8,128)(2,1)} %bitcast.4, bf16[128,2432]{1,0:T(8,128)(2,1)} %pos_hbm.1, bf16[2,1800,2432]{2,1,0:T(8,128)(2,1)} %bitcast.3, bf16[2,600,2432]{2,1,0:T(8,128)(2,1)} %wout_hbm.1), custom_call_target="tpu_custom_call" | custom-call | tf_op jit(solution)/shard_map/music_rows/pallas_call | solution.py:296
  49.0 0.8 %copy.7 = bf16[128,2432]{1,0:T(8,128)(2,1)} copy(bf16[128,2432]{1,0:T(8,128)(2,1)S(1)} %music_rows.1) | data formatting | bytes 1245184

commit v3 on v2

--- a/solution.py
+++ b/solution.py
@@ -197,33 +197,51 @@
             mixed[src * cols:(src + 1) * cols, a:b] = mix_r[part][src].astype(jnp.float32)
 
     loads[3].wait()
-    for parts in ((0,), tuple(range(1, len(mix)))):
-        for part in parts:
-            receive_mix(part)
-        lo, hi = mix[parts[0]][0], mix[parts[-1]][1]
+    for part, (lo, hi) in enumerate(mix):
+        receive_mix(part)
         back = mixed[:, lo:hi].astype(jnp.bfloat16)
+        shift_by, first_sum, second_sum = None, None, None
         for a, b in cuts(depth, 512):
-            resid[:, a:b] += jnp.dot(back, wo_v[0, lo:hi, a:b], preferred_element_type=jnp.float32)
-    normalize_into(resid, normed)
-
-    def shift(part):
+            value = resid[:, a:b] + jnp.dot(back, wo_v[0, lo:hi, a:b], preferred_element_type=jnp.float32)
+            resid[:, a:b] = value
+            if part < len(mix) - 1:
+                continue
+            if shift_by is None:
+                shift_by = jnp.mean(value[:, :128], axis=-1, keepdims=True)
+                first_sum = jnp.zeros((tokens, 128), jnp.float32)
+                second_sum = jnp.zeros((tokens, 128), jnp.float32)
+            for c in range(0, b - a, 128):
+                off = value[:, c:c + 128] - shift_by
+                first_sum += off
+                second_sum += off * off
+    off_mean = jnp.sum(first_sum, axis=-1, keepdims=True) * (1.0 / depth)
+    variance = jnp.sum(second_sum, axis=-1, keepdims=True) * (1.0 / depth) - off_mean * off_mean
+    scale = lax.rsqrt(variance + epsilon)
+    center = shift_by + off_mean
+    for a, b in cuts(depth, 512):
+        normed[:, a:b] = ((resid[:, a:b] - center) * scale).astype(jnp.bfloat16)
+
+    def shift(kind, head):
         return pltpu.make_async_remote_copy(
-            src_ref=kv_s[part], dst_ref=kv_r[part], send_sem=kv_ss.at[part], recv_sem=kv_rs.at[part],
+            src_ref=kv_s[kind].at[head], dst_ref=kv_r[kind].at[head],
+            send_sem=kv_ss.at[kind, head], recv_sem=kv_rs.at[kind, head],
             device_id={"seq": lax.rem(me + 1, n)}, device_id_type=MESH)
 
     @pl.when(me == 0)
     def _():
-        for part in range(HEADS):
-            kv_r[part][...] = jnp.zeros_like(kv_r[part])
-
-    for part, (a, b) in enumerate(head_spans(width)):
+        for kind in range(2):
+            kv_r[kind][...] = jnp.zeros_like(kv_r[kind])
+
+    for head, (a, b) in enumerate(head_spans(width)):
         wide[:, a:b] = jnp.dot(normed[...], wt[:, a:b], preferred_element_type=jnp.float32)
-        at = 3 * HEAD * part + HEAD
-        kv_s[part][...] = wide[:, at:at + 2 * HEAD].astype(jnp.bfloat16)
+        for kind in range(2):
+            at = 3 * HEAD * head + HEAD * (kind + 1)
+            kv_s[kind][head] = wide[:, at:at + HEAD].T.astype(jnp.bfloat16)
 
         @pl.when(me < n - 1)
         def _():
-            shift(part).start()
+            for kind in range(2):
+                shift(kind, head).start()
 
     owns = []
     for h in range(HEADS):
@@ -234,32 +252,35 @@
         owns.append(own)
 
     loads[5].wait()
+    pieces = spans([0] + [HEAD * h // 128 * 128 for h in range(2, HEADS)] + [att])
     for h in range(HEADS):
         @pl.when(me > 0)
         def _():
-            shift(h).wait_recv()
+            shift(0, h).wait_recv()
         at = 3 * HEAD * h
         q = wide[:, at:at + HEAD].astype(jnp.bfloat16)
         v_own = wide[:, at + 2 * HEAD:at + 3 * HEAD].astype(jnp.bfloat16).astype(jnp.float32)
-        k = kv_r[h][:, :HEAD]
-        v = kv_r[h][:, HEAD:]
         own = owns[h]
-        far = jnp.where(me > 0, scores_of(q, k), -jnp.inf)
+        far = jnp.where(me > 0, jnp.dot(q, kv_r[0][h], preferred_element_type=jnp.float32) * inv_root, -jnp.inf)
         top = jnp.maximum(jnp.max(far, axis=-1, keepdims=True), own)
         far_lifted = jnp.exp(far - top)
         own_lifted = jnp.exp(own - top)
-        total = jnp.sum(far_lifted, axis=-1, keepdims=True) + own_lifted
-        far_probs = (far_lifted / total).astype(jnp.bfloat16)
-        own_probs = (own_lifted / total).astype(jnp.bfloat16).astype(jnp.float32)
-        mixed[:, HEAD * h:HEAD * (h + 1)] = (
-            jnp.dot(far_probs, v, preferred_element_type=jnp.float32) + own_probs * v_own)
-        if h == 1:
-            lo, hi = mix[0]
+        share = 1.0 / (jnp.sum(far_lifted, axis=-1, keepdims=True) + own_lifted)
+        far_probs = (far_lifted * share).astype(jnp.bfloat16)
+        own_probs = (own_lifted * share).astype(jnp.bfloat16).astype(jnp.float32)
+        own_part = own_probs * v_own
+        if h >= 2:
+            lo, hi = pieces[h - 2]
             back = mixed[:, lo:hi].astype(jnp.bfloat16)
             for a, b in cuts(depth, 512):
                 resid[:, a:b] += jnp.dot(back, wo_v[1, lo:hi, a:b], preferred_element_type=jnp.float32)
 
-    lo, hi = mix[1][0], mix[-1][1]
+        @pl.when(me > 0)
+        def _():
+            shift(1, h).wait_recv()
+        mixed[:, HEAD * h:HEAD * (h + 1)] = dot_nt(far_probs, kv_r[1][h]) + own_part
+
+    lo, hi = pieces[-1]
     back = mixed[:, lo:hi].astype(jnp.bfloat16)
     for a, b in cuts(depth, 512):
         out_ref[:, a:b] = (resid[:, a:b] + jnp.dot(
@@ -274,8 +295,9 @@
 
     @pl.when(me < n - 1)
     def _():
-        for part in range(HEADS):
-            shift(part).wait_send()
+        for kind in range(2):
+            for head in range(HEADS):
+                shift(kind, head).wait_send()
 
 
 def solution(mesh):
@@ -291,7 +313,7 @@
         hbm = pl.BlockSpec(memory_space=pl.ANY)
         qkv = [pltpu.VMEM((n, cols, b - a), bf16) for a, b in qkv_spans(width)]
         mix = [pltpu.VMEM((n, cols, b - a), bf16) for a, b in mix_spans(att)]
-        kv = [pltpu.VMEM((tokens, 2 * HEAD), bf16)] * HEADS
+        kv = [pltpu.VMEM((HEADS, HEAD, tokens), bf16)] * 2
         sems = pltpu.SemaphoreType.DMA
         return pl.pallas_call(
             functools.partial(kernel, n),
@@ -318,7 +340,7 @@
                 sems((7,)),
                 sems, sems((n,)), sems, sems,
                 sems((len(qkv),)), sems((len(qkv),)), sems((len(mix),)), sems((len(mix),)),
-                sems((HEADS,)), sems((HEADS,)),
+                sems((2, HEADS)), sems((2, HEADS)),
             ],
             compiler_params=pltpu.CompilerParams(
                 collective_id=0, has_side_effects=True, vmem_limit_bytes=56 << 20),

time: 50 us -> 48.9 us (0.978)
  Pallas kernels: 49 us -> 47.7 us
    pallas_call x1, Pallas kernels: 49 us -> 47.7 us  [shards(): pl.pallas_call(functools.partial(kernel, n), out_shape=pltpu.VMEM((tokens...]
where the time goes in v3:
time: 48.9 us; the launch traced here: 48.5 us
  Pallas kernels  47.7 us (98%)
  local copies, waits for them, and re-layouts  0.83 us (2%)
    pallas_call x1, Pallas kernels, shards(): pl.pallas_call(functools.partial(kernel, n), out_shape=pltpu.VMEM((tokens...  47.7 us

profile of v3, /device:TPU:12, one launch (start us, length us, event | category | flops | bytes accessed | tf_op | source)
XLA Modules:
  0.0 48.5 jit_solution(14797078578544454197)
XLA Ops:
  0.0 47.7 %music_rows.1 = bf16[128,2432]{1,0:T(8,128)(2,1)S(1)} custom-call(s32[1,128]{1,0:T(1,128)} %bitcast.5, bf16[152,2048]{1,0:T(8,128)(2,1)} %bitcast.4, bf16[128,2432]{1,0:T(8,128)(2,1)} %pos_hbm.1, bf16[2,1800,2432]{2,1,0:T(8,128)(2,1)} %bitcast.3, bf16[2,600,2432]{2,1,0:T(8,128)(2,1)} %wout_hbm.1), custom_call_target="tpu_custom_call" | custom-call | tf_op jit(solution)/shard_map/music_rows/pallas_call | solution.py:318
  47.7 0.8 %copy.7 = bf16[128,2432]{1,0:T(8,128)(2,1)} copy(bf16[128,2432]{1,0:T(8,128)(2,1)S(1)} %music_rows.1) | data formatting | bytes 1245184

commit v4 on v3

--- a/solution.py
+++ b/solution.py
@@ -30,11 +30,11 @@
 
 def qkv_spans(width):
     heads = head_spans(width)
-    return [(heads[h][0], heads[h + 1][1]) for h in range(0, HEADS, 2)]
+    return [(0, heads[1][1])] + heads[2:]
 
 
 def mix_spans(att):
-    return spans([0, 2 * HEAD // 128 * 128, att])
+    return spans([0, 2 * HEAD // 128 * 128, 3 * HEAD // 128 * 128, att])
 
 
 def normalize_into(resid, normed):
@@ -107,7 +107,7 @@
 
     def serve(step, carry):
         group, turn = step // (n // 2), lax.rem(step, n // 2)
-        k = 2 * lax.rem(turn + n // 4, n // 2) + (group ^ parity)
+        k = 2 * (n // 2 - 1 - turn) + (group ^ parity)
         peer = me ^ k
 
         @pl.when(k > 0)
@@ -167,8 +167,8 @@
     mix = mix_spans(att)
     sent = 0
     for h in range(HEADS):
-        if h % 2 == 0:
-            part = h // 2
+        if h != 1:
+            part = max(h - 1, 0)
             a, b = qkv[part]
             settle_all(qkv_r[part], qkv_rs.at[part])
             for src in range(n):
@@ -179,7 +179,7 @@
         v = wide[:, at + 2 * HEAD:at + 3 * HEAD].astype(jnp.bfloat16)
         scores = jnp.where(allowed, scores_of(q, k), -jnp.inf)
         lifted = jnp.exp(scores - jnp.max(scores, axis=-1, keepdims=True))
-        probs = (lifted / jnp.sum(lifted, axis=-1, keepdims=True)).astype(jnp.bfloat16)
+        probs = (lifted * (1.0 / jnp.sum(lifted, axis=-1, keepdims=True))).astype(jnp.bfloat16)
         mixed[:, HEAD * h:HEAD * (h + 1)] = jnp.dot(probs, v, preferred_element_type=jnp.float32)
         while sent < len(mix) and mix[sent][1] <= HEAD * (h + 1):
             a, b = mix[sent]

time: 48.9 us -> 47.9 us (0.980)
  Pallas kernels: 47.7 us -> 46.5 us
    pallas_call x1, Pallas kernels: 47.7 us -> 46.5 us  [shards(): pl.pallas_call(functools.partial(kernel, n), out_shape=pltpu.VMEM((tokens...]
where the time goes in v4:
time: 47.9 us; the launch traced here: 47.3 us
  Pallas kernels  46.5 us (97%)
  local copies, waits for them, and re-layouts  0.83 us (2%)
    pallas_call x1, Pallas kernels, shards(): pl.pallas_call(functools.partial(kernel, n), out_shape=pltpu.VMEM((tokens...  46.5 us

profile of v4, /device:TPU:12, one launch (start us, length us, event | category | flops | bytes accessed | tf_op | source)
XLA Modules:
  0.0 47.3 jit_solution(10635755285241576130)
XLA Ops:
  0.0 46.5 %music_rows.1 = bf16[128,2432]{1,0:T(8,128)(2,1)S(1)} custom-call(s32[1,128]{1,0:T(1,128)} %bitcast.5, bf16[152,2048]{1,0:T(8,128)(2,1)} %bitcast.4, bf16[128,2432]{1,0:T(8,128)(2,1)} %pos_hbm.1, bf16[2,1800,2432]{2,1,0:T(8,128)(2,1)} %bitcast.3, bf16[2,600,2432]{2,1,0:T(8,128)(2,1)} %wout_hbm.1), custom_call_target="tpu_custom_call" | custom-call | tf_op jit(solution)/shard_map/music_rows/pallas_call | solution.py:318
  46.5 0.8 %copy.7 = bf16[128,2432]{1,0:T(8,128)(2,1)} copy(bf16[128,2432]{1,0:T(8,128)(2,1)S(1)} %music_rows.1) | data formatting | bytes 1245184

commit v5 on v4

--- a/solution.py
+++ b/solution.py
@@ -94,7 +94,7 @@
     ids_load.wait()
     pl.semaphore_wait(barrier, n - 1)
 
-    for k in others:
+    for k in range(n - 1, 0, -1):
         send(own_ids, own_ids, ids_ss, ids_rs.at[k], k).start()
     loads[0].wait()
     for load in loads[1:]:

time: 47.9 us -> 47.8 us (level)
  no operation moved by 1% of the time
where the time goes in v5:
time: 47.8 us; the launch traced here: 47.2 us
  Pallas kernels  46.4 us (97%)
  local copies, waits for them, and re-layouts  0.83 us (2%)
    pallas_call x1, Pallas kernels, shards(): pl.pallas_call(functools.partial(kernel, n), out_shape=pltpu.VMEM((tokens...  46.4 us

profile of v5, /device:TPU:12, one launch (start us, length us, event | category | flops | bytes accessed | tf_op | source)
XLA Modules:
  0.0 47.2 jit_solution(12972301909065268201)
XLA Ops:
  0.0 46.4 %music_rows.1 = bf16[128,2432]{1,0:T(8,128)(2,1)S(1)} custom-call(s32[1,128]{1,0:T(1,128)} %bitcast.5, bf16[152,2048]{1,0:T(8,128)(2,1)} %bitcast.4, bf16[128,2432]{1,0:T(8,128)(2,1)} %pos_hbm.1, bf16[2,1800,2432]{2,1,0:T(8,128)(2,1)} %bitcast.3, bf16[2,600,2432]{2,1,0:T(8,128)(2,1)} %wout_hbm.1), custom_call_target="tpu_custom_call" | custom-call | tf_op jit(solution)/shard_map/music_rows/pallas_call | solution.py:318
  46.4 0.8 %copy.7 = bf16[128,2432]{1,0:T(8,128)(2,1)} copy(bf16[128,2432]{1,0:T(8,128)(2,1)S(1)} %music_rows.1) | data formatting | bytes 1245184
